TPU v7x, 32 devices: a whole 2x2x4 slice. The times are simulated.
32 devices in a mesh: inst: 2 (over y), cell: 16 (over z, x, core).
Axes of the slice: x: 2, y: 2, z: 4, core: 2. Of those that a mesh axis runs over, the one named last changes fastest.
Arguments:
- adjoint: bfloat16 [4, 5, 32, 16, 256], P('inst', None, 'cell'), may hold values from -6 to 6
- flux_jac: bfloat16 [4, 5, 3, 32, 16, 256], P('inst', None, None, 'cell'), may hold values from -1.25 to 1.25
- shift: float32 [32, 16, 256], P('cell', 'inst'), may hold values from 0.1 to 2
Outputs:
- mesh_adjoint: float32 [3, 32, 16, 256], P(None, 'cell', 'inst')
- residual: float32 [3, 32, 16, 256], P(None, 'cell', 'inst')
All inputs are finite; a program needn't handle non-finite values.
Results may differ from a plain program's by a relative error of at most 0.0003.
Values may be sent and summed in bfloat16 or wider, within the bound.
A program may use at most 64 MiB of HBM per device.

v0:
```python
import jax
import jax.numpy as jnp
from jax import lax
from jax.sharding import PartitionSpec as P

ITERS = 3
mu_shear = 1.0
lame_first = 1.5


def padded_2(block, sides, width):
    for axis, dim in sides:
        count = lax.axis_size(axis)
        forward = [(i, i + 1) for i in range(count - 1)]
        backward = [(target, source) for source, target in forward]
        low = lax.ppermute(
            lax.slice_in_dim(block, block.shape[dim] - width, None, axis=dim), axis, forward
        )
        high = lax.ppermute(lax.slice_in_dim(block, 0, width, axis=dim), axis, backward)
        block = jnp.concatenate([low, block, high], axis=dim)
    return block


def operate(field, shift):
    padded = padded_2(field, (("inst", 2), ("cell", 1)), 1)
    padded = jnp.pad(padded, ((0, 0), (0, 0), (0, 0), (1, 1)))
    center = padded[:, 1:-1, 1:-1, 1:-1]
    beside = padded[:, 2:, 1:-1, 1:-1] + padded[:, :-2, 1:-1, 1:-1]
    beside = beside + padded[:, 1:-1, 2:, 1:-1] + padded[:, 1:-1, :-2, 1:-1]
    beside = beside + padded[:, 1:-1, 1:-1, 2:] + padded[:, 1:-1, 1:-1, :-2]
    corner = padded[:, :-1, :-1, :-1]
    diverge = (
        padded[0, 1:, :-1, :-1]
        - corner[0]
        + (padded[1, :-1, 1:, :-1] - corner[1])
        + (padded[2, :-1, :-1, 1:] - corner[2])
    )
    cell_first = lax.axis_index("cell") == 0
    inst_first = lax.axis_index("inst") == 0
    keep_rows = jnp.where((jnp.arange(diverge.shape[0]) == 0) & cell_first, 0.0, 1.0).astype(
        jnp.float32
    )
    keep_cols = jnp.where((jnp.arange(diverge.shape[1]) == 0) & inst_first, 0.0, 1.0).astype(
        jnp.float32
    )
    keep_depth = jnp.where(jnp.arange(diverge.shape[2]) == 0, 0.0, 1.0).astype(jnp.float32)
    diverge = (
        diverge * keep_rows[:, None, None] * keep_cols[None, :, None] * keep_depth[None, None, :]
    )
    inner = diverge[1:, 1:, 1:]
    grad_part = jnp.stack(
        [diverge[:-1, 1:, 1:] - inner, diverge[1:, :-1, 1:] - inner, diverge[1:, 1:, :-1] - inner]
    )
    return mu_shear * (6.0 * center - beside) + shift * center + lame_first * grad_part


def two_products(residual, image):
    return lax.psum((jnp.sum(residual * residual), jnp.sum(residual * image)), ("inst", "cell"))


def local(adjoint, flux_jac, shift):
    padded = padded_2(adjoint, (("cell", 2),), 1)
    upper = jnp.einsum(
        "ivkxyz,ivxyz->kxyz", flux_jac, padded[:, :, 2:], preferred_element_type=jnp.float32
    )
    lower = jnp.einsum(
        "ivkxyz,ivxyz->kxyz", flux_jac, padded[:, :, :-2], preferred_element_type=jnp.float32
    )
    partial_sum = upper - lower
    block_cols = shift.shape[1]
    totals = lax.psum(partial_sum, "inst")
    sens = lax.dynamic_slice_in_dim(totals, lax.axis_index("inst") * block_cols, block_cols, 2)
    mesh_adjoint = jnp.zeros_like(sens)
    residual = sens
    image = operate(residual, shift)
    norm_now, product = two_products(residual, image)
    alpha = norm_now / product
    direction, along = (residual, image)
    for sweep in range(ITERS):
        mesh_adjoint = mesh_adjoint + alpha * direction
        residual = residual - alpha * along
        if sweep + 1 < ITERS:
            image = operate(residual, shift)
            norm_next, product = two_products(residual, image)
            ratio = norm_next / norm_now
            alpha = norm_next / (product - ratio * norm_next / alpha)
            direction = residual + ratio * direction
            along = image + ratio * along
            norm_now = norm_next
    return (mesh_adjoint, residual)


def solution(mesh):
    placed = (
        P("inst", None, "cell", None, None),
        P("inst", None, None, "cell", None, None),
        P("cell", "inst", None),
    )
    return jax.shard_map(
        local,
        mesh=mesh,
        in_specs=placed,
        out_specs=(P(None, "cell", "inst", None), P(None, "cell", "inst", None)),
        check_vma=False,
    )
```

profile of v0, /device:TPU:0, one launch (start us, length us, event | category | flops | bytes accessed | tf_op | source)
XLA Modules:
  0.0 234.0 jit_solution(14785577434391238408)
XLA Ops:
  7.2 0.0 all-reduce.8.cloned.1.call-start
  7.2 1.0 fusion.56
  8.2 1.3 collective-permute-start
  9.5 3.0 %collective-permute-start.1 = (bf16[2,5,1,16,256]{4,3,2,1,0:T(8,128)(2,1)S(1)}, bf16[2,5,1,16,256]{4,3,2,1,0:T(8,128)(2,1)S(1)}, u32[]{:S(2)}, u32[]{:S(2)}) collective-permute-start(bf16[2,5,1,16,256]{4,3,2,1,0:T(8,128)(2,1)S(1)} %get-tuple-element.22), channel_id=1, source_target_pairs={{0,1},{1,2},{2,3},{3,4},{4,5},{5,6},{6,7},{7,8},{8,9},{9,10},{10,1... | collective-permute-start | bytes 245768 | tf_op jit(solution)/shard_map/ppermute | solution.py:16
  12.6 0.9 collective-permute-done.1
  13.5 0.1 copy-done.1
  13.6 0.2 fusion.1
  13.8 0.7 subtract_bitcast_fusion
  14.5 27.2 %all-reduce.8.cloned.1.call-done = f32[3,2,16,256]{3,2,1,0:T(8,128)} async-done(((f32[3,2,16,256]{3,2,1,0:T(8,128)}), f32[3,2,16,256]{3,2,1,0:T(8,128)}) %all-reduce.8.cloned.1.call-update) | async-done | bytes 98320 | tf_op jit(solution)/shard_map/psum | solution.py:71
  41.6 0.9 constant_dynamic-slice_fusion.1
  42.5 2.1 collective-permute-start.2
  44.6 1.3 collective-permute-start.3
  45.9 0.8 constant_dynamic-slice_fusion.2
  46.7 3.4 %collective-permute-done.3 = f32[3,2,1,256]{3,2,1,0:T(1,128)S(1)} collective-permute-done((f32[3,2,1,256]{3,2,1,0:T(1,128)S(1)}, f32[3,2,1,256]{3,2,1,0:T(1,128)S(1)}, u32[]{:S(2)}, u32[]{:S(2)}) %collective-permute-start.3) | collective-permute-done | bytes 6176 | tf_op jit(solution)/shard_map/ppermute | solution.py:19
  50.2 1.3 collective-permute-start.4
  51.5 3.0 %collective-permute-start.5 = (f32[3,1,10,256]{3,2,1,0:T(8,128)S(1)}, f32[3,1,10,256]{3,2,1,0:T(8,128)S(1)}, u32[]{:S(2)}, u32[]{:S(2)}) collective-permute-start(f32[3,1,10,256]{3,2,1,0:T(8,128)S(1)} %get-tuple-element.27), channel_id=1, source_target_pairs={{0,1},{1,2},{2,3},{3,4},{4,5},{5,6},{6,7},{7,8},{8,9},{9,10},{10,1... | collective-permute-start | bytes 92168 | tf_op jit(solution)/shard_map/ppermute | solution.py:16
  54.5 0.8 collective-permute-done.5
  55.4 0.2 select_maximum_fusion.8
  55.6 0.1 fusion.23
  55.7 0.1 fusion.51
  55.8 0.6 copy-done.3
  56.4 0.7 multiply_reduce_fusion.4
  57.1 43.0 %all-reduce.5 = (f32[]{:T(128)}, f32[]{:T(128)}) all-reduce(f32[]{:T(128)} %get-tuple-element.9, f32[]{:T(128)} %get-tuple-element.8), channel_id=1, replica_groups=mesh['inst'=2,'cell'=16] {'inst','cell'}, use_global_device_ids=true, to_apply=%region_2.3 | all-reduce | flops 2 | bytes 16 | tf_op jit(solution)/shard_map/psum | solution.py:58
  101.4 4.4 %collective-permute-start.6 = (f32[3,2,1,256]{3,2,1,0:T(1,128)S(1)}, f32[3,2,1,256]{3,2,1,0:T(1,128)S(1)}, u32[]{:S(2)}, u32[]{:S(2)}) collective-permute-start(f32[3,2,1,256]{3,2,1,0:T(1,128)S(1)} %get-tuple-element.44), channel_id=1, source_target_pairs={{0,16},{1,17},{2,18},{3,19},{4,20},{5,21},{6,22},{7,23},{8,24},{9,... | collective-permute-start | bytes 18440 | tf_op jit(solution)/shard_map/ppermute | solution.py:16
  105.8 1.3 collective-permute-start.7
  107.1 0.0 collective-permute-done.6
  107.1 4.2 %collective-permute-done.7 = f32[3,2,1,256]{3,2,1,0:T(1,128)S(1)} collective-permute-done((f32[3,2,1,256]{3,2,1,0:T(1,128)S(1)}, f32[3,2,1,256]{3,2,1,0:T(1,128)S(1)}, u32[]{:S(2)}, u32[]{:S(2)}) %collective-permute-start.7) | collective-permute-done | bytes 6176 | tf_op jit(solution)/shard_map/ppermute | solution.py:19
  111.4 1.3 collective-permute-start.8
  112.7 3.0 %collective-permute-start.9 = (f32[3,1,10,256]{3,2,1,0:T(8,128)S(1)}, f32[3,1,10,256]{3,2,1,0:T(8,128)S(1)}, u32[]{:S(2)}, u32[]{:S(2)}) collective-permute-start(f32[3,1,10,256]{3,2,1,0:T(8,128)S(1)} %get-tuple-element.25), channel_id=1, source_target_pairs={{0,1},{1,2},{2,3},{3,4},{4,5},{5,6},{6,7},{7,8},{8,9},{9,10},{10,1... | collective-permute-start | bytes 92168 | tf_op jit(solution)/shard_map/ppermute | solution.py:16
  115.7 0.9 collective-permute-done.9
  116.6 0.2 select_maximum_fusion.4
  116.8 0.1 fusion.17
  116.9 0.1 fusion.48
  117.0 0.7 multiply_reduce_fusion.2
  117.7 42.4 %all-reduce.4 = (f32[]{:T(128)}, f32[]{:T(128)}) all-reduce(f32[]{:T(128)} %get-tuple-element.7, f32[]{:T(128)} %get-tuple-element.6), channel_id=1, replica_groups=mesh['inst'=2,'cell'=16] {'inst','cell'}, use_global_device_ids=true, to_apply=%region_6.7 | all-reduce | flops 2 | bytes 16 | tf_op jit(solution)/shard_map/psum | solution.py:58
  164.7 4.4 %collective-permute-start.10 = (f32[3,2,1,256]{3,2,1,0:T(1,128)S(1)}, f32[3,2,1,256]{3,2,1,0:T(1,128)S(1)}, u32[]{:S(2)}, u32[]{:S(2)}) collective-permute-start(f32[3,2,1,256]{3,2,1,0:T(1,128)S(1)} %get-tuple-element.42), channel_id=1, source_target_pairs={{0,16},{1,17},{2,18},{3,19},{4,20},{5,21},{6,22},{7,23},{8,24},{9,... | collective-permute-start | bytes 18440 | tf_op jit(solution)/shard_map/ppermute | solution.py:16
  169.2 1.3 collective-permute-start.11
  170.5 0.0 collective-permute-done.10
  170.5 4.2 %collective-permute-done.11 = f32[3,2,1,256]{3,2,1,0:T(1,128)S(1)} collective-permute-done((f32[3,2,1,256]{3,2,1,0:T(1,128)S(1)}, f32[3,2,1,256]{3,2,1,0:T(1,128)S(1)}, u32[]{:S(2)}, u32[]{:S(2)}) %collective-permute-start.11) | collective-permute-done | bytes 6176 | tf_op jit(solution)/shard_map/ppermute | solution.py:19
  174.8 1.3 collective-permute-start.12
  176.1 3.0 %collective-permute-start.13 = (f32[3,1,10,256]{3,2,1,0:T(8,128)S(1)}, f32[3,1,10,256]{3,2,1,0:T(8,128)S(1)}, u32[]{:S(2)}, u32[]{:S(2)}) collective-permute-start(f32[3,1,10,256]{3,2,1,0:T(8,128)S(1)} %get-tuple-element.23), channel_id=1, source_target_pairs={{0,1},{1,2},{2,3},{3,4},{4,5},{5,6},{6,7},{7,8},{8,9},{9,10},{10,1... | collective-permute-start | bytes 92168 | tf_op jit(solution)/shard_map/ppermute | solution.py:16
  179.1 0.9 collective-permute-done.13
  180.0 0.2 select_maximum_fusion
  180.2 0.1 fusion.11
  180.3 0.1 fusion.45
  180.3 0.7 multiply_reduce_fusion
  181.0 41.4 %all-reduce.3 = (f32[]{:T(128)}, f32[]{:T(128)}) all-reduce(f32[]{:T(128)} %get-tuple-element.5, f32[]{:T(128)} %get-tuple-element.4), channel_id=1, replica_groups=mesh['inst'=2,'cell'=16] {'inst','cell'}, use_global_device_ids=true, to_apply=%region_10.11 | all-reduce | flops 2 | bytes 16 | tf_op jit(solution)/shard_map/psum | solution.py:58
  226.5 0.7 multiply_subtract_fusion
  (26 shorter events, 0.3 us)
Async XLA Ops:
  7.2 6.3 %copy-start = (bf16[2,5,2,16,256]{4,3,2,1,0:T(8,128)(2,1)S(1)}, bf16[2,5,2,16,256]{4,3,2,1,0:T(8,128)(2,1)}, u32[]{:S(2)}) copy-start(bf16[2,5,2,16,256]{4,3,2,1,0:T(8,128)(2,1)} %param.3) | copy-start | bytes 491524
  7.2 34.5 %all-reduce.8.cloned.1.call-start = ((), (), s32[]{:S(2)}) async-start(), calls=%async_computation | async-start | bytes 196608 | tf_op jit(solution)/shard_map/psum | solution.py:71
  8.2 4.4 %collective-permute-start = (bf16[2,5,1,16,256]{4,3,2,1,0:T(8,128)(2,1)S(1)}, bf16[2,5,1,16,256]{4,3,2,1,0:T(8,128)(2,1)S(1)}, u32[]{:S(2)}, u32[]{:S(2)}) collective-permute-start(bf16[2,5,1,16,256]{4,3,2,1,0:T(8,128)(2,1)S(1)} %get-tuple-element.21), channel_id=1, source_target_pairs={{1,0},{2,1},{3,2},{4,3},{5,4},{6,5},{7,6},{8,7},{9,8},{10,9},{11,1... | collective-permute-start | bytes 245768 | tf_op jit(solution)/shard_map/ppermute | solution.py:19
  9.5 3.9 %collective-permute-start.1 = (bf16[2,5,1,16,256]{4,3,2,1,0:T(8,128)(2,1)S(1)}, bf16[2,5,1,16,256]{4,3,2,1,0:T(8,128)(2,1)S(1)}, u32[]{:S(2)}, u32[]{:S(2)}) collective-permute-start(bf16[2,5,1,16,256]{4,3,2,1,0:T(8,128)(2,1)S(1)} %get-tuple-element.22), channel_id=1, source_target_pairs={{0,1},{1,2},{2,3},{3,4},{4,5},{5,6},{6,7},{7,8},{8,9},{9,10},{10,1... | collective-permute-start | bytes 245768 | tf_op jit(solution)/shard_map/ppermute | solution.py:16
  12.6 1.0 copy-start.1
  42.5 4.2 %collective-permute-start.2 = (f32[3,2,1,256]{3,2,1,0:T(1,128)S(1)}, f32[3,2,1,256]{3,2,1,0:T(1,128)S(1)}, u32[]{:S(2)}, u32[]{:S(2)}) collective-permute-start(f32[3,2,1,256]{3,2,1,0:T(1,128)S(1)} %get-tuple-element.29), channel_id=1, source_target_pairs={{0,16},{1,17},{2,18},{3,19},{4,20},{5,21},{6,22},{7,23},{8,24},{9,... | collective-permute-start | bytes 18440 | tf_op jit(solution)/shard_map/ppermute | solution.py:16
  44.6 5.5 %collective-permute-start.3 = (f32[3,2,1,256]{3,2,1,0:T(1,128)S(1)}, f32[3,2,1,256]{3,2,1,0:T(1,128)S(1)}, u32[]{:S(2)}, u32[]{:S(2)}) collective-permute-start(f32[3,2,1,256]{3,2,1,0:T(1,128)S(1)} %get-tuple-element.30), channel_id=1, source_target_pairs={{16,0},{17,1},{18,2},{19,3},{20,4},{21,5},{22,6},{23,7},{24,8},{25... | collective-permute-start | bytes 18440 | tf_op jit(solution)/shard_map/ppermute | solution.py:19
  50.2 4.4 %collective-permute-start.4 = (f32[3,1,10,256]{3,2,1,0:T(8,128)S(1)}, f32[3,1,10,256]{3,2,1,0:T(8,128)S(1)}, u32[]{:S(2)}, u32[]{:S(2)}) collective-permute-start(f32[3,1,10,256]{3,2,1,0:T(8,128)S(1)} %get-tuple-element.28), channel_id=1, source_target_pairs={{1,0},{2,1},{3,2},{4,3},{5,4},{6,5},{7,6},{8,7},{9,8},{10,9},{11,1... | collective-permute-start | bytes 92168 | tf_op jit(solution)/shard_map/ppermute | solution.py:19
  51.5 3.9 %collective-permute-start.5 = (f32[3,1,10,256]{3,2,1,0:T(8,128)S(1)}, f32[3,1,10,256]{3,2,1,0:T(8,128)S(1)}, u32[]{:S(2)}, u32[]{:S(2)}) collective-permute-start(f32[3,1,10,256]{3,2,1,0:T(8,128)S(1)} %get-tuple-element.27), channel_id=1, source_target_pairs={{0,1},{1,2},{2,3},{3,4},{4,5},{5,6},{6,7},{7,8},{8,9},{9,10},{10,1... | collective-permute-start | bytes 92168 | tf_op jit(solution)/shard_map/ppermute | solution.py:16
  55.7 0.7 copy-start.3
  56.4 45.0 %copy-start.2 = (f32[3,2,16,256]{3,2,1,0:T(8,128)S(1)}, f32[3,2,16,256]{3,2,1,0:T(8,128)}, u32[]{:S(2)}) copy-start(f32[3,2,16,256]{3,2,1,0:T(8,128)} %all-reduce.8.cloned.1.call-done) | copy-start | bytes 294916
  101.4 5.7 %collective-permute-start.6 = (f32[3,2,1,256]{3,2,1,0:T(1,128)S(1)}, f32[3,2,1,256]{3,2,1,0:T(1,128)S(1)}, u32[]{:S(2)}, u32[]{:S(2)}) collective-permute-start(f32[3,2,1,256]{3,2,1,0:T(1,128)S(1)} %get-tuple-element.44), channel_id=1, source_target_pairs={{0,16},{1,17},{2,18},{3,19},{4,20},{5,21},{6,22},{7,23},{8,24},{9,... | collective-permute-start | bytes 18440 | tf_op jit(solution)/shard_map/ppermute | solution.py:16
  105.8 5.5 %collective-permute-start.7 = (f32[3,2,1,256]{3,2,1,0:T(1,128)S(1)}, f32[3,2,1,256]{3,2,1,0:T(1,128)S(1)}, u32[]{:S(2)}, u32[]{:S(2)}) collective-permute-start(f32[3,2,1,256]{3,2,1,0:T(1,128)S(1)} %get-tuple-element.45), channel_id=1, source_target_pairs={{16,0},{17,1},{18,2},{19,3},{20,4},{21,5},{22,6},{23,7},{24,8},{25... | collective-permute-start | bytes 18440 | tf_op jit(solution)/shard_map/ppermute | solution.py:19
  111.4 4.3 %collective-permute-start.8 = (f32[3,1,10,256]{3,2,1,0:T(8,128)S(1)}, f32[3,1,10,256]{3,2,1,0:T(8,128)S(1)}, u32[]{:S(2)}, u32[]{:S(2)}) collective-permute-start(f32[3,1,10,256]{3,2,1,0:T(8,128)S(1)} %get-tuple-element.26), channel_id=1, source_target_pairs={{1,0},{2,1},{3,2},{4,3},{5,4},{6,5},{7,6},{8,7},{9,8},{10,9},{11,1... | collective-permute-start | bytes 92168 | tf_op jit(solution)/shard_map/ppermute | solution.py:19
  112.7 3.9 %collective-permute-start.9 = (f32[3,1,10,256]{3,2,1,0:T(8,128)S(1)}, f32[3,1,10,256]{3,2,1,0:T(8,128)S(1)}, u32[]{:S(2)}, u32[]{:S(2)}) collective-permute-start(f32[3,1,10,256]{3,2,1,0:T(8,128)S(1)} %get-tuple-element.25), channel_id=1, source_target_pairs={{0,1},{1,2},{2,3},{3,4},{4,5},{5,6},{6,7},{7,8},{8,9},{9,10},{10,1... | collective-permute-start | bytes 92168 | tf_op jit(solution)/shard_map/ppermute | solution.py:16
  164.7 5.8 %collective-permute-start.10 = (f32[3,2,1,256]{3,2,1,0:T(1,128)S(1)}, f32[3,2,1,256]{3,2,1,0:T(1,128)S(1)}, u32[]{:S(2)}, u32[]{:S(2)}) collective-permute-start(f32[3,2,1,256]{3,2,1,0:T(1,128)S(1)} %get-tuple-element.42), channel_id=1, source_target_pairs={{0,16},{1,17},{2,18},{3,19},{4,20},{5,21},{6,22},{7,23},{8,24},{9,... | collective-permute-start | bytes 18440 | tf_op jit(solution)/shard_map/ppermute | solution.py:16
  169.2 5.5 %collective-permute-start.11 = (f32[3,2,1,256]{3,2,1,0:T(1,128)S(1)}, f32[3,2,1,256]{3,2,1,0:T(1,128)S(1)}, u32[]{:S(2)}, u32[]{:S(2)}) collective-permute-start(f32[3,2,1,256]{3,2,1,0:T(1,128)S(1)} %get-tuple-element.43), channel_id=1, source_target_pairs={{16,0},{17,1},{18,2},{19,3},{20,4},{21,5},{22,6},{23,7},{24,8},{25... | collective-permute-start | bytes 18440 | tf_op jit(solution)/shard_map/ppermute | solution.py:19
  174.8 4.3 %collective-permute-start.12 = (f32[3,1,10,256]{3,2,1,0:T(8,128)S(1)}, f32[3,1,10,256]{3,2,1,0:T(8,128)S(1)}, u32[]{:S(2)}, u32[]{:S(2)}) collective-permute-start(f32[3,1,10,256]{3,2,1,0:T(8,128)S(1)} %get-tuple-element.24), channel_id=1, source_target_pairs={{1,0},{2,1},{3,2},{4,3},{5,4},{6,5},{7,6},{8,7},{9,8},{10,9},{11,1... | collective-permute-start | bytes 92168 | tf_op jit(solution)/shard_map/ppermute | solution.py:19
  176.1 3.9 %collective-permute-start.13 = (f32[3,1,10,256]{3,2,1,0:T(8,128)S(1)}, f32[3,1,10,256]{3,2,1,0:T(8,128)S(1)}, u32[]{:S(2)}, u32[]{:S(2)}) collective-permute-start(f32[3,1,10,256]{3,2,1,0:T(8,128)S(1)} %get-tuple-element.23), channel_id=1, source_target_pairs={{0,1},{1,2},{2,3},{3,4},{4,5},{5,6},{6,7},{7,8},{8,9},{9,10},{10,1... | collective-permute-start | bytes 92168 | tf_op jit(solution)/shard_map/ppermute | solution.py:16
Sparse Core Ops, SparseCore 0:
  14.6 27.0 all-reduce.7
where the time goes:
time: 235 us; the launch traced here: 234 us
  blocking collectives  127 us (54%)
  waiting for transfers between devices  42.5 us (18%)
  starting transfers between devices  32.1 us (14%)
  between operations  24.4 us (10%)
  other arithmetic  4.82 us (2%)
  local copies, waits for them, and re-layouts  3.46 us (1%)
    psum x3, blocking collectives, two_products(): lax.psum((jnp.sum(residual * residual), jnp.sum(residual * image)), ('ins...  127 us
    psum x1, waiting for transfers between devices, local(): totals = lax.psum(partial_sum, 'inst')  27.2 us
    ppermute x7, starting transfers between devices, padded_2(): lax.ppermute(lax.slice_in_dim(block, block.shape[dim] - width, None, axis...  23 us
    ppermute x7, waiting for transfers between devices, padded_2(): lax.ppermute(lax.slice_in_dim(block, 0, width, axis=dim), axis, backward)  11.8 us
    ppermute x7, starting transfers between devices, padded_2(): lax.ppermute(lax.slice_in_dim(block, 0, width, axis=dim), axis, backward)  9.04 us
  transfers between devices with their start and end apart: 15, of which 8 were waited for; matrix products, arithmetic and copies ran while one was open for 0% of the time, Pallas kernels for 0%

commit v1 on v0

--- a/solution.py
+++ b/solution.py
@@ -68,7 +68,7 @@
     )
     partial_sum = upper - lower
     block_cols = shift.shape[1]
-    totals = lax.psum(partial_sum, "inst")
+    totals = jnp.sum(lax.all_gather(partial_sum, "inst"), axis=0)
     sens = lax.dynamic_slice_in_dim(totals, lax.axis_index("inst") * block_cols, block_cols, 2)
     mesh_adjoint = jnp.zeros_like(sens)
     residual = sens

time: 235 us -> 205 us (0.87)
  waiting for transfers between devices: 42.5 us -> 16 us
  between operations: 24.4 us -> 10.8 us
  blocking collectives: 127 us -> 136 us
    psum x1 -> x0, waiting for transfers between devices: 27.2 us -> none  [local(): totals = lax.psum(partial_sum, 'inst')]
    all_gather x0 -> x1, blocking collectives: none -> 6.25 us  [local(): totals = jnp.sum(lax.all_gather(partial_sum, 'inst'), axis=0)]
    psum x3, blocking collectives: 127 us -> 130 us  [two_products(): lax.psum((jnp.sum(residual * residual), jnp.sum(residual * image)), ('ins...]
  transfers between devices with their start and end apart: 15 -> 14, of which waited for: 8 -> 7; matrix products, arithmetic and copies ran while one was open for 0% -> 0% of each run, Pallas kernels for 0% -> 0%
where the time goes in v1:
time: 205 us; the launch traced here: 204 us
  blocking collectives  136 us (66%)
  starting transfers between devices  34.4 us (17%)
  waiting for transfers between devices  16 us (8%)
  between operations  10.8 us (5%)
  other arithmetic  4.22 us (2%)
    psum x3, blocking collectives, two_products(): lax.psum((jnp.sum(residual * residual), jnp.sum(residual * image)), ('ins...  130 us
    ppermute x7, starting transfers between devices, padded_2(): lax.ppermute(lax.slice_in_dim(block, block.shape[dim] - width, None, axis...  25.3 us
    ppermute x7, waiting for transfers between devices, padded_2(): lax.ppermute(lax.slice_in_dim(block, 0, width, axis=dim), axis, backward)  12.6 us
    ppermute x7, starting transfers between devices, padded_2(): lax.ppermute(lax.slice_in_dim(block, 0, width, axis=dim), axis, backward)  9.04 us
    all_gather x1, blocking collectives, local(): totals = jnp.sum(lax.all_gather(partial_sum, 'inst'), axis=0)  6.25 us
  transfers between devices with their start and end apart: 14, of which 7 were waited for; matrix products, arithmetic and copies ran while one was open for 0% of the time, Pallas kernels for 0%

profile of v1, /device:TPU:0, one launch (start us, length us, event | category | flops | bytes accessed | tf_op | source)
XLA Modules:
  0.0 203.6 jit_solution(17624733312936412429)
XLA Ops:
  0.6 1.0 fusion.56
  1.6 1.3 collective-permute-start
  2.9 3.0 %collective-permute-start.1 = (bf16[2,5,1,16,256]{4,3,2,1,0:T(8,128)(2,1)S(1)}, bf16[2,5,1,16,256]{4,3,2,1,0:T(8,128)(2,1)S(1)}, u32[]{:S(2)}, u32[]{:S(2)}) collective-permute-start(bf16[2,5,1,16,256]{4,3,2,1,0:T(8,128)(2,1)S(1)} %get-tuple-element.22), channel_id=1, source_target_pairs={{0,1},{1,2},{2,3},{3,4},{4,5},{5,6},{6,7},{7,8},{8,9},{9,10},{10,1... | collective-permute-start | bytes 245768 | tf_op jit(solution)/shard_map/ppermute | solution.py:16
  6.0 0.0 copy-start.1
  6.0 0.8 collective-permute-done.1
  6.9 0.1 copy-done.1
  7.0 0.2 fusion.1
  7.2 6.3 %all-gather = f32[6,2,16,256]{3,2,1,0:T(8,128)S(1)} all-gather(f32[3,2,16,256]{3,2,1,0:T(8,128)S(1)} %subtract_bitcast_fusion), channel_id=2, replica_groups=mesh['inst'=2,'cell'=16] {'inst'}, dimensions={0}, use_global_device_ids=true | all-gather | bytes 294912 | tf_op jit(solution)/shard_map/all_gather | solution.py:71
  13.5 4.4 %collective-permute-start.2 = (f32[3,2,1,256]{3,2,1,0:T(1,128)S(1)}, f32[3,2,1,256]{3,2,1,0:T(1,128)S(1)}, u32[]{:S(2)}, u32[]{:S(2)}) collective-permute-start(f32[3,2,1,256]{3,2,1,0:T(1,128)S(1)} %get-tuple-element.29), channel_id=1, source_target_pairs={{0,16},{1,17},{2,18},{3,19},{4,20},{5,21},{6,22},{7,23},{8,24},{9,... | collective-permute-start | bytes 18440 | tf_op jit(solution)/shard_map/ppermute | solution.py:16
  17.9 1.3 collective-permute-start.3
  19.3 0.0 collective-permute-done.2
  19.3 4.2 %collective-permute-done.3 = f32[3,2,1,256]{3,2,1,0:T(1,128)S(1)} collective-permute-done((f32[3,2,1,256]{3,2,1,0:T(1,128)S(1)}, f32[3,2,1,256]{3,2,1,0:T(1,128)S(1)}, u32[]{:S(2)}, u32[]{:S(2)}) %collective-permute-start.3) | collective-permute-done | bytes 6176 | tf_op jit(solution)/shard_map/ppermute | solution.py:19
  23.5 1.3 collective-permute-start.4
  24.8 3.0 %collective-permute-start.5 = (f32[3,1,10,256]{3,2,1,0:T(8,128)S(1)}, f32[3,1,10,256]{3,2,1,0:T(8,128)S(1)}, u32[]{:S(2)}, u32[]{:S(2)}) collective-permute-start(f32[3,1,10,256]{3,2,1,0:T(8,128)S(1)} %get-tuple-element.27), channel_id=1, source_target_pairs={{0,1},{1,2},{2,3},{3,4},{4,5},{5,6},{6,7},{7,8},{8,9},{9,10},{10,1... | collective-permute-start | bytes 92168 | tf_op jit(solution)/shard_map/ppermute | solution.py:16
  27.9 0.8 collective-permute-done.5
  28.7 0.2 select_maximum_fusion.8
  28.9 0.1 fusion.23
  29.0 0.0 copy-start.2
  29.0 0.1 fusion.51
  29.1 0.6 copy-done.2
  29.7 0.7 multiply_reduce_fusion.4
  30.4 46.4 %all-reduce.5 = (f32[]{:T(128)}, f32[]{:T(128)}) all-reduce(f32[]{:T(128)} %get-tuple-element.9, f32[]{:T(128)} %get-tuple-element.8), channel_id=1, replica_groups=mesh['inst'=2,'cell'=16] {'inst','cell'}, use_global_device_ids=true, to_apply=%region_2.3 | all-reduce | flops 2 | bytes 16 | tf_op jit(solution)/shard_map/psum | solution.py:58
  78.2 4.4 %collective-permute-start.6 = (f32[3,2,1,256]{3,2,1,0:T(1,128)S(1)}, f32[3,2,1,256]{3,2,1,0:T(1,128)S(1)}, u32[]{:S(2)}, u32[]{:S(2)}) collective-permute-start(f32[3,2,1,256]{3,2,1,0:T(1,128)S(1)} %get-tuple-element.44), channel_id=1, source_target_pairs={{0,16},{1,17},{2,18},{3,19},{4,20},{5,21},{6,22},{7,23},{8,24},{9,... | collective-permute-start | bytes 18440 | tf_op jit(solution)/shard_map/ppermute | solution.py:16
  82.5 1.3 collective-permute-start.7
  83.8 0.0 collective-permute-done.6
  83.9 4.2 %collective-permute-done.7 = f32[3,2,1,256]{3,2,1,0:T(1,128)S(1)} collective-permute-done((f32[3,2,1,256]{3,2,1,0:T(1,128)S(1)}, f32[3,2,1,256]{3,2,1,0:T(1,128)S(1)}, u32[]{:S(2)}, u32[]{:S(2)}) %collective-permute-start.7) | collective-permute-done | bytes 6176 | tf_op jit(solution)/shard_map/ppermute | solution.py:19
  88.1 1.3 collective-permute-start.8
  89.4 3.0 %collective-permute-start.9 = (f32[3,1,10,256]{3,2,1,0:T(8,128)S(1)}, f32[3,1,10,256]{3,2,1,0:T(8,128)S(1)}, u32[]{:S(2)}, u32[]{:S(2)}) collective-permute-start(f32[3,1,10,256]{3,2,1,0:T(8,128)S(1)} %get-tuple-element.25), channel_id=1, source_target_pairs={{0,1},{1,2},{2,3},{3,4},{4,5},{5,6},{6,7},{7,8},{8,9},{9,10},{10,1... | collective-permute-start | bytes 92168 | tf_op jit(solution)/shard_map/ppermute | solution.py:16
  92.4 0.0 collective-permute-done.8
  92.5 0.9 collective-permute-done.9
  93.3 0.2 select_maximum_fusion.4
  93.5 0.1 fusion.17
  93.6 0.1 fusion.48
  93.7 0.7 multiply_reduce_fusion.2
  94.4 42.4 %all-reduce.4 = (f32[]{:T(128)}, f32[]{:T(128)}) all-reduce(f32[]{:T(128)} %get-tuple-element.7, f32[]{:T(128)} %get-tuple-element.6), channel_id=1, replica_groups=mesh['inst'=2,'cell'=16] {'inst','cell'}, use_global_device_ids=true, to_apply=%region_6.7 | all-reduce | flops 2 | bytes 16 | tf_op jit(solution)/shard_map/psum | solution.py:58
  141.4 4.4 %collective-permute-start.10 = (f32[3,2,1,256]{3,2,1,0:T(1,128)S(1)}, f32[3,2,1,256]{3,2,1,0:T(1,128)S(1)}, u32[]{:S(2)}, u32[]{:S(2)}) collective-permute-start(f32[3,2,1,256]{3,2,1,0:T(1,128)S(1)} %get-tuple-element.42), channel_id=1, source_target_pairs={{0,16},{1,17},{2,18},{3,19},{4,20},{5,21},{6,22},{7,23},{8,24},{9,... | collective-permute-start | bytes 18440 | tf_op jit(solution)/shard_map/ppermute | solution.py:16
  145.8 1.3 collective-permute-start.11
  147.1 0.0 collective-permute-done.10
  147.1 4.2 %collective-permute-done.11 = f32[3,2,1,256]{3,2,1,0:T(1,128)S(1)} collective-permute-done((f32[3,2,1,256]{3,2,1,0:T(1,128)S(1)}, f32[3,2,1,256]{3,2,1,0:T(1,128)S(1)}, u32[]{:S(2)}, u32[]{:S(2)}) %collective-permute-start.11) | collective-permute-done | bytes 6176 | tf_op jit(solution)/shard_map/ppermute | solution.py:19
  151.4 1.3 collective-permute-start.12
  152.7 3.0 %collective-permute-start.13 = (f32[3,1,10,256]{3,2,1,0:T(8,128)S(1)}, f32[3,1,10,256]{3,2,1,0:T(8,128)S(1)}, u32[]{:S(2)}, u32[]{:S(2)}) collective-permute-start(f32[3,1,10,256]{3,2,1,0:T(8,128)S(1)} %get-tuple-element.23), channel_id=1, source_target_pairs={{0,1},{1,2},{2,3},{3,4},{4,5},{5,6},{6,7},{7,8},{8,9},{9,10},{10,1... | collective-permute-start | bytes 92168 | tf_op jit(solution)/shard_map/ppermute | solution.py:16
  155.7 0.9 collective-permute-done.13
  156.6 0.2 select_maximum_fusion
  156.8 0.1 fusion.11
  156.9 0.1 fusion.45
  157.0 0.7 multiply_reduce_fusion
  157.7 41.4 %all-reduce.3 = (f32[]{:T(128)}, f32[]{:T(128)}) all-reduce(f32[]{:T(128)} %get-tuple-element.5, f32[]{:T(128)} %get-tuple-element.4), channel_id=1, replica_groups=mesh['inst'=2,'cell'=16] {'inst','cell'}, use_global_device_ids=true, to_apply=%region_10.11 | all-reduce | flops 2 | bytes 16 | tf_op jit(solution)/shard_map/psum | solution.py:58
  203.0 0.7 multiply_subtract_fusion
  (23 shorter events, 0.3 us)
Async XLA Ops:
  0.6 6.2 %copy-start = (bf16[2,5,2,16,256]{4,3,2,1,0:T(8,128)(2,1)S(1)}, bf16[2,5,2,16,256]{4,3,2,1,0:T(8,128)(2,1)}, u32[]{:S(2)}) copy-start(bf16[2,5,2,16,256]{4,3,2,1,0:T(8,128)(2,1)} %param.3) | copy-start | bytes 491524
  1.6 4.4 %collective-permute-start = (bf16[2,5,1,16,256]{4,3,2,1,0:T(8,128)(2,1)S(1)}, bf16[2,5,1,16,256]{4,3,2,1,0:T(8,128)(2,1)S(1)}, u32[]{:S(2)}, u32[]{:S(2)}) collective-permute-start(bf16[2,5,1,16,256]{4,3,2,1,0:T(8,128)(2,1)S(1)} %get-tuple-element.21), channel_id=1, source_target_pairs={{1,0},{2,1},{3,2},{4,3},{5,4},{6,5},{7,6},{8,7},{9,8},{10,9},{11,1... | collective-permute-start | bytes 245768 | tf_op jit(solution)/shard_map/ppermute | solution.py:19
  2.9 3.9 %collective-permute-start.1 = (bf16[2,5,1,16,256]{4,3,2,1,0:T(8,128)(2,1)S(1)}, bf16[2,5,1,16,256]{4,3,2,1,0:T(8,128)(2,1)S(1)}, u32[]{:S(2)}, u32[]{:S(2)}) collective-permute-start(bf16[2,5,1,16,256]{4,3,2,1,0:T(8,128)(2,1)S(1)} %get-tuple-element.22), channel_id=1, source_target_pairs={{0,1},{1,2},{2,3},{3,4},{4,5},{5,6},{6,7},{7,8},{8,9},{9,10},{10,1... | collective-permute-start | bytes 245768 | tf_op jit(solution)/shard_map/ppermute | solution.py:16
  6.0 1.0 copy-start.1
  13.5 5.7 %collective-permute-start.2 = (f32[3,2,1,256]{3,2,1,0:T(1,128)S(1)}, f32[3,2,1,256]{3,2,1,0:T(1,128)S(1)}, u32[]{:S(2)}, u32[]{:S(2)}) collective-permute-start(f32[3,2,1,256]{3,2,1,0:T(1,128)S(1)} %get-tuple-element.29), channel_id=1, source_target_pairs={{0,16},{1,17},{2,18},{3,19},{4,20},{5,21},{6,22},{7,23},{8,24},{9,... | collective-permute-start | bytes 18440 | tf_op jit(solution)/shard_map/ppermute | solution.py:16
  17.9 5.5 %collective-permute-start.3 = (f32[3,2,1,256]{3,2,1,0:T(1,128)S(1)}, f32[3,2,1,256]{3,2,1,0:T(1,128)S(1)}, u32[]{:S(2)}, u32[]{:S(2)}) collective-permute-start(f32[3,2,1,256]{3,2,1,0:T(1,128)S(1)} %get-tuple-element.30), channel_id=1, source_target_pairs={{16,0},{17,1},{18,2},{19,3},{20,4},{21,5},{22,6},{23,7},{24,8},{25... | collective-permute-start | bytes 18440 | tf_op jit(solution)/shard_map/ppermute | solution.py:19
  23.5 4.4 %collective-permute-start.4 = (f32[3,1,10,256]{3,2,1,0:T(8,128)S(1)}, f32[3,1,10,256]{3,2,1,0:T(8,128)S(1)}, u32[]{:S(2)}, u32[]{:S(2)}) collective-permute-start(f32[3,1,10,256]{3,2,1,0:T(8,128)S(1)} %get-tuple-element.28), channel_id=1, source_target_pairs={{1,0},{2,1},{3,2},{4,3},{5,4},{6,5},{7,6},{8,7},{9,8},{10,9},{11,1... | collective-permute-start | bytes 92168 | tf_op jit(solution)/shard_map/ppermute | solution.py:19
  24.8 3.9 %collective-permute-start.5 = (f32[3,1,10,256]{3,2,1,0:T(8,128)S(1)}, f32[3,1,10,256]{3,2,1,0:T(8,128)S(1)}, u32[]{:S(2)}, u32[]{:S(2)}) collective-permute-start(f32[3,1,10,256]{3,2,1,0:T(8,128)S(1)} %get-tuple-element.27), channel_id=1, source_target_pairs={{0,1},{1,2},{2,3},{3,4},{4,5},{5,6},{6,7},{7,8},{8,9},{9,10},{10,1... | collective-permute-start | bytes 92168 | tf_op jit(solution)/shard_map/ppermute | solution.py:16
  29.0 0.7 copy-start.2
  78.2 5.7 %collective-permute-start.6 = (f32[3,2,1,256]{3,2,1,0:T(1,128)S(1)}, f32[3,2,1,256]{3,2,1,0:T(1,128)S(1)}, u32[]{:S(2)}, u32[]{:S(2)}) collective-permute-start(f32[3,2,1,256]{3,2,1,0:T(1,128)S(1)} %get-tuple-element.44), channel_id=1, source_target_pairs={{0,16},{1,17},{2,18},{3,19},{4,20},{5,21},{6,22},{7,23},{8,24},{9,... | collective-permute-start | bytes 18440 | tf_op jit(solution)/shard_map/ppermute | solution.py:16
  82.5 5.5 %collective-permute-start.7 = (f32[3,2,1,256]{3,2,1,0:T(1,128)S(1)}, f32[3,2,1,256]{3,2,1,0:T(1,128)S(1)}, u32[]{:S(2)}, u32[]{:S(2)}) collective-permute-start(f32[3,2,1,256]{3,2,1,0:T(1,128)S(1)} %get-tuple-element.45), channel_id=1, source_target_pairs={{16,0},{17,1},{18,2},{19,3},{20,4},{21,5},{22,6},{23,7},{24,8},{25... | collective-permute-start | bytes 18440 | tf_op jit(solution)/shard_map/ppermute | solution.py:19
  88.1 4.3 %collective-permute-start.8 = (f32[3,1,10,256]{3,2,1,0:T(8,128)S(1)}, f32[3,1,10,256]{3,2,1,0:T(8,128)S(1)}, u32[]{:S(2)}, u32[]{:S(2)}) collective-permute-start(f32[3,1,10,256]{3,2,1,0:T(8,128)S(1)} %get-tuple-element.26), channel_id=1, source_target_pairs={{1,0},{2,1},{3,2},{4,3},{5,4},{6,5},{7,6},{8,7},{9,8},{10,9},{11,1... | collective-permute-start | bytes 92168 | tf_op jit(solution)/shard_map/ppermute | solution.py:19
  89.4 3.9 %collective-permute-start.9 = (f32[3,1,10,256]{3,2,1,0:T(8,128)S(1)}, f32[3,1,10,256]{3,2,1,0:T(8,128)S(1)}, u32[]{:S(2)}, u32[]{:S(2)}) collective-permute-start(f32[3,1,10,256]{3,2,1,0:T(8,128)S(1)} %get-tuple-element.25), channel_id=1, source_target_pairs={{0,1},{1,2},{2,3},{3,4},{4,5},{5,6},{6,7},{7,8},{8,9},{9,10},{10,1... | collective-permute-start | bytes 92168 | tf_op jit(solution)/shard_map/ppermute | solution.py:16
  141.4 5.8 %collective-permute-start.10 = (f32[3,2,1,256]{3,2,1,0:T(1,128)S(1)}, f32[3,2,1,256]{3,2,1,0:T(1,128)S(1)}, u32[]{:S(2)}, u32[]{:S(2)}) collective-permute-start(f32[3,2,1,256]{3,2,1,0:T(1,128)S(1)} %get-tuple-element.42), channel_id=1, source_target_pairs={{0,16},{1,17},{2,18},{3,19},{4,20},{5,21},{6,22},{7,23},{8,24},{9,... | collective-permute-start | bytes 18440 | tf_op jit(solution)/shard_map/ppermute | solution.py:16
  145.8 5.5 %collective-permute-start.11 = (f32[3,2,1,256]{3,2,1,0:T(1,128)S(1)}, f32[3,2,1,256]{3,2,1,0:T(1,128)S(1)}, u32[]{:S(2)}, u32[]{:S(2)}) collective-permute-start(f32[3,2,1,256]{3,2,1,0:T(1,128)S(1)} %get-tuple-element.43), channel_id=1, source_target_pairs={{16,0},{17,1},{18,2},{19,3},{20,4},{21,5},{22,6},{23,7},{24,8},{25... | collective-permute-start | bytes 18440 | tf_op jit(solution)/shard_map/ppermute | solution.py:19
  151.4 4.3 %collective-permute-start.12 = (f32[3,1,10,256]{3,2,1,0:T(8,128)S(1)}, f32[3,1,10,256]{3,2,1,0:T(8,128)S(1)}, u32[]{:S(2)}, u32[]{:S(2)}) collective-permute-start(f32[3,1,10,256]{3,2,1,0:T(8,128)S(1)} %get-tuple-element.24), channel_id=1, source_target_pairs={{1,0},{2,1},{3,2},{4,3},{5,4},{6,5},{7,6},{8,7},{9,8},{10,9},{11,1... | collective-permute-start | bytes 92168 | tf_op jit(solution)/shard_map/ppermute | solution.py:19
  152.7 3.9 %collective-permute-start.13 = (f32[3,1,10,256]{3,2,1,0:T(8,128)S(1)}, f32[3,1,10,256]{3,2,1,0:T(8,128)S(1)}, u32[]{:S(2)}, u32[]{:S(2)}) collective-permute-start(f32[3,1,10,256]{3,2,1,0:T(8,128)S(1)} %get-tuple-element.23), channel_id=1, source_target_pairs={{0,1},{1,2},{2,3},{3,4},{4,5},{5,6},{6,7},{7,8},{8,9},{9,10},{10,1... | collective-permute-start | bytes 92168 | tf_op jit(solution)/shard_map/ppermute | solution.py:16
